TPU v7x, 32 devices: a whole 2x2x4 slice. The times are simulated.
32 devices in a mesh: blk: 8 (over z, x), rep: 4 (over y, core).
Axes of the slice: x: 2, y: 2, z: 4, core: 2. Of those that a mesh axis runs over, the one named last changes fastest.
Arguments:
- points: bfloat16 [6144, 1024], P('blk'), may hold values from -6 to 6
- w_in: bfloat16 [1024, 512], replicated, may hold values from -0.1875 to 0.1875
- b_in: float32 [512], replicated, may hold values from -3 to 3
- w_out: bfloat16 [512, 64], replicated, may hold values from -0.25 to 0.25
- inv_scale: float32 [64], replicated, may hold values from 0.05 to 0.5
- solves: bfloat16 [64, 6144], P(None, 'blk'), may hold values from -1.6875 to 1.6875
- probes: bfloat16 [64, 6144], P(None, 'blk'), may hold values from -1.6875 to 1.6875
Outputs:
- feat_grad: float32 [64, 6144], P(None, ('blk', 'rep'))
- grad_w_in: float32 [1024, 512], replicated
- grad_b_in: float32 [512], replicated
- grad_w_out: float32 [512, 64], replicated
All inputs are finite; a program needn't handle non-finite values.
Results may differ from a plain program's by a relative error of at most 0.034.
Values may be sent and summed in bfloat16 or wider, within the bound.
No kernel may reach another device: no remote copies, remote signals or barrier semaphores. Data moves between devices by JAX's collectives and lax.ppermute only.
A program may use at most 64 MiB of HBM per device.

v0:
```python
import math
import jax
import jax.numpy as jnp
from jax import lax
from jax.sharding import PartitionSpec as P


def shifted(block, axis, distance):
    devices = range(lax.axis_size(axis))
    route = [((i - distance) % len(devices), i) for i in devices]
    return lax.ppermute(block, axis, route)


def couple(own_y, own_pair, own_sq, visitor, feat):
    vis_y = visitor[:feat]
    vis_pair = visitor[feat:]
    vis_sq = jnp.sum(jnp.square(vis_y.astype(jnp.float32)), axis=0)
    cross = lax.dot_general(
        own_y, vis_y, (((0,), (0,)), ((), ())), preferred_element_type=jnp.float32
    )
    kernel = jnp.exp(-0.5 * (own_sq[:, None] + vis_sq[None, :] - 2.0 * cross))
    coupling = lax.dot_general(
        own_pair, vis_pair, (((0,), (0,)), ((), ())), preferred_element_type=jnp.float32
    )
    weight_b = (coupling * kernel).astype(jnp.bfloat16)
    totals = jnp.sum(weight_b.astype(jnp.float32), axis=1)
    pull = lax.dot_general(
        vis_y, weight_b, (((1,), (1,)), ((), ())), preferred_element_type=jnp.float32
    )
    return (totals, pull)


def on_device(points, w_in, b_in, w_out, inv_scale, solves, probes):
    feat = w_out.shape[1]
    reps = lax.axis_size("rep")
    blocks = lax.axis_size("blk")
    rep_index = lax.axis_index("rep")
    rows = points.shape[0]
    quarter = rows // reps
    first = rep_index * quarter
    npts = rows * blocks
    levels = reps.bit_length() - 1
    own_points = lax.dynamic_slice_in_dim(points, first, quarter, 0)
    hidden = jnp.tanh(jnp.dot(points, w_in, preferred_element_type=jnp.float32) + b_in).astype(
        jnp.bfloat16
    )
    pre = lax.dot_general(
        w_out, hidden, (((0,), (1,)), ((), ())), preferred_element_type=jnp.float32
    )
    hidden, scaled = (hidden, (pre * inv_scale[:, None]).astype(jnp.bfloat16))
    own_hidden = lax.dynamic_slice_in_dim(hidden, first, quarter, 0)
    own_pair = jnp.concatenate([solves, probes], axis=0)
    own_sq = jnp.sum(jnp.square(scaled.astype(jnp.float32)), axis=0)
    scaled32 = scaled.astype(jnp.float32)
    visitor = jnp.concatenate([scaled, probes, solves], axis=0)
    for bit in range(levels):
        moved = shifted(visitor, "blk", -(1 << bit))
        visitor = jnp.where(rep_index // (1 << bit) % 2 == 1, moved, visitor)

    def accumulate(state, vis):
        totals, pull = couple(scaled, own_pair, own_sq, vis, feat)
        return (state[0] + totals, state[1] + pull)

    init = (jnp.zeros((rows,), jnp.float32), jnp.zeros((feat, rows), jnp.float32))
    steps = blocks // reps

    def advance(index, carry):
        state, vis = carry
        state = accumulate(state, vis)
        return (state, shifted(vis, "blk", -reps))

    state, last_vis = lax.fori_loop(0, steps - 1, advance, (init, visitor))
    state = accumulate(state, last_vis)
    totals, pull = state
    drift = pull - scaled32 * totals[None, :]
    summed = lax.psum_scatter(drift, "rep", scatter_dimension=1, tiled=True)
    feat_grad = summed * inv_scale[:, None]
    grad_b16 = feat_grad.astype(jnp.bfloat16)
    back = lax.dot_general(
        grad_b16, w_out, (((0,), (1,)), ((), ())), preferred_element_type=jnp.float32
    )
    hid32 = own_hidden.astype(jnp.float32)
    pre_grad = back * (1.0 - hid32 * hid32)
    norm = 1.0 / math.sqrt(npts)
    term_w_in = (
        lax.dot_general(
            own_points,
            pre_grad.astype(jnp.bfloat16),
            (((0,), (0,)), ((), ())),
            preferred_element_type=jnp.float32,
        )
        * norm
    )
    term_b_in = jnp.sum(pre_grad, axis=0) * norm
    term_w_out = (
        lax.dot_general(
            own_hidden, grad_b16, (((0,), (1,)), ((), ())), preferred_element_type=jnp.float32
        )
        * norm
    )
    grad_w_in, grad_b_in, grad_w_out = lax.psum((term_w_in, term_b_in, term_w_out), ("blk", "rep"))
    return (feat_grad, grad_w_in, grad_b_in, grad_w_out)


def solution(mesh):
    in_specs = (P("blk", None), P(), P(), P(), P(), P(None, "blk"), P(None, "blk"))
    out_specs = (P(None, ("blk", "rep")), P(), P(), P())
    return jax.shard_map(
        on_device, mesh=mesh, in_specs=in_specs, out_specs=out_specs, check_vma=False
    )
```

profile of v0, /device:TPU:0, one launch (start us, length us, event | category | flops | bytes accessed | tf_op | source)
XLA Modules:
  0.0 224.5 jit_solution(10279714449616067677)
XLA Ops:
  7.2 0.0 copy-start
  7.2 0.0 reduce-scatter.4.cloned.1.call-start
  7.3 1.3 copy-done
  8.6 2.2 tanh_convert_fusion
  10.8 0.4 fusion.3
  11.2 6.1 %collective-permute-start = (bf16[192,768]{1,0:T(8,128)(2,1)S(1)}, bf16[192,768]{1,0:T(8,128)(2,1)S(1)}, u32[]{:S(2)}, u32[]{:S(2)}) collective-permute-start(bf16[192,768]{1,0:T(8,128)(2,1)S(1)} %pad_maximum_fusion), channel_id=1, source_target_pairs={{4,0},{8,4},{12,8},{16,12},{20,16},{24,20},{28,24},{0,28},{5,1},{9... | collective-permute-start | bytes 884744 | tf_op jit(solution)/shard_map/ppermute | solution.py:11
  17.3 6.3 %collective-permute-done = bf16[192,768]{1,0:T(8,128)(2,1)S(1)} collective-permute-done((bf16[192,768]{1,0:T(8,128)(2,1)S(1)}, bf16[192,768]{1,0:T(8,128)(2,1)S(1)}, u32[]{:S(2)}, u32[]{:S(2)}) %collective-permute-start) | collective-permute-done | bytes 294944 | tf_op jit(solution)/shard_map/ppermute | solution.py:11
  23.6 0.1 broadcast_select_fusion
  23.6 1.6 collective-permute-start.1
  25.3 6.3 %collective-permute-done.1 = bf16[192,768]{1,0:T(8,128)(2,1)S(1)} collective-permute-done((bf16[192,768]{1,0:T(8,128)(2,1)S(1)}, bf16[192,768]{1,0:T(8,128)(2,1)S(1)}, u32[]{:S(2)}, u32[]{:S(2)}) %collective-permute-start.1) | collective-permute-done | bytes 294944 | tf_op jit(solution)/shard_map/ppermute | solution.py:11
  31.6 0.6 collective-permute-start.2
  32.3 0.5 fusion.13
  32.8 0.9 convert_reduce_fusion.1
  33.7 12.2 %collective-permute-done.2 = bf16[192,768]{1,0:T(8,128)(2,1)S(1)} collective-permute-done((bf16[192,768]{1,0:T(8,128)(2,1)S(1)}, bf16[192,768]{1,0:T(8,128)(2,1)S(1)}, u32[]{:S(2)}, u32[]{:S(2)}) %collective-permute-start.2) | collective-permute-done | bytes 294944 | tf_op jit(solution)/shard_map/while/body/eval_jaxpr/ppermute | solution.py:11
  46.0 0.5 fusion.10
  46.5 0.9 convert_reduce_fusion
  47.4 0.3 fusion.8
  47.8 0.3 fusion
  48.1 0.9 copy.11
  49.0 0.0 reduce-scatter.4.cloned.1.call-update
  49.1 0.0 all-reduce.3.cloned.1.call-start
  49.1 22.9 %reduce-scatter.4.cloned.1.call-done = f32[192,64]{1,0:T(8,128)} async-done(((f32[768,64]{1,0:T(8,128)}), f32[192,64]{1,0:T(8,128)}) %reduce-scatter.4.cloned.1.call-update) | async-done | bytes 49168
  72.0 1.0 copy.12
  73.0 0.1 broadcast_multiply_fusion
  73.0 0.3 fusion.19
  73.3 0.8 convolution_multiply_fusion.3
  74.1 1.8 convolution_multiply_fusion
  75.9 0.0 all-reduce.3.cloned.1.call-update
  76.0 39.6 %psum.22 = f32[512]{0:T(512)} all-reduce(f32[512]{0:T(512)S(1)} %broadcast_multiply_fusion.1), channel_id=1, replica_groups=mesh['blk'=8,'rep'=4] {'blk','rep'}, use_global_device_ids=true, to_apply=%region_8.9 | all-reduce | flops 512 | bytes 4096 | tf_op jit(solution)/shard_map/psum | solution.py:101
  115.6 98.3 %all-reduce.3.cloned.1.call-done = (f32[1024,512]{1,0:T(8,128)}, f32[512,64]{0,1:T(8,128)}) async-done(((f32[1024,512]{1,0:T(8,128)}, f32[512,64]{0,1:T(8,128)}), (f32[1024,512]{1,0:T(8,128)}, f32[512,64]{0,1:T(8,128)})) %all-reduce.3.cloned.1.call-update) | async-done | bytes 2228240 | tf_op jit(solution)/shard_map/psum | solution.py:101
  213.9 3.1 %copy.16 = f32[1024,512]{1,0:T(8,128)} copy(f32[1024,512]{1,0:T(8,128)} %get-tuple-element.38) | data formatting | bytes 4194304
  217.0 0.7 copy.17
  (20 shorter events, 0.2 us)
Async XLA Ops:
  7.2 1.4 copy-start
  7.2 3.6 %copy-start.6 = (f32[64]{0:T(128)S(1)}, f32[64]{0:T(128)}, u32[]{:S(2)}) copy-start(f32[64]{0:T(128)} %param.11) | copy-start | bytes 772
  7.2 3.6 %copy-start.5 = (bf16[512,64]{0,1:T(8,128)(2,1)S(1)}, bf16[512,64]{0,1:T(8,128)(2,1)}, u32[]{:S(2)}) copy-start(bf16[512,64]{0,1:T(8,128)(2,1)} %param.10) | copy-start | bytes 196612
  7.2 4.0 %copy-start.1 = (bf16[64,768]{1,0:T(8,128)(2,1)S(1)}, bf16[64,768]{1,0:T(8,128)(2,1)}, u32[]{:S(2)}) copy-start(bf16[64,768]{1,0:T(8,128)(2,1)} %param.12) | copy-start | bytes 294916
  7.2 4.0 %copy-start.2 = (bf16[64,768]{1,0:T(8,128)(2,1)S(1)}, bf16[64,768]{1,0:T(8,128)(2,1)}, u32[]{:S(2)}) copy-start(bf16[64,768]{1,0:T(8,128)(2,1)} %param.13) | copy-start | bytes 294916
  7.2 64.8 %reduce-scatter.4.cloned.1.call-start = ((), (), s32[]{:S(2)}) async-start(), calls=%async_computation.1 | async-start | bytes 491520
  11.2 12.3 %collective-permute-start = (bf16[192,768]{1,0:T(8,128)(2,1)S(1)}, bf16[192,768]{1,0:T(8,128)(2,1)S(1)}, u32[]{:S(2)}, u32[]{:S(2)}) collective-permute-start(bf16[192,768]{1,0:T(8,128)(2,1)S(1)} %pad_maximum_fusion), channel_id=1, source_target_pairs={{4,0},{8,4},{12,8},{16,12},{20,16},{24,20},{28,24},{0,28},{5,1},{9... | collective-permute-start | bytes 884744 | tf_op jit(solution)/shard_map/ppermute | solution.py:11
  23.6 7.9 %collective-permute-start.1 = (bf16[192,768]{1,0:T(8,128)(2,1)S(1)}, bf16[192,768]{1,0:T(8,128)(2,1)S(1)}, u32[]{:S(2)}, u32[]{:S(2)}) collective-permute-start(bf16[192,768]{1,0:T(8,128)(2,1)S(1)} %broadcast_select_fusion), channel_id=1, source_target_pairs={{8,0},{12,4},{16,8},{20,12},{24,16},{28,20},{0,24},{4,28},{9,1},{1... | collective-permute-start | bytes 884744 | tf_op jit(solution)/shard_map/ppermute | solution.py:11
  31.6 14.3 %collective-permute-start.2 = (bf16[192,768]{1,0:T(8,128)(2,1)S(1)}, bf16[192,768]{1,0:T(8,128)(2,1)S(1)}, u32[]{:S(2)}, u32[]{:S(2)}) collective-permute-start(bf16[192,768]{1,0:T(8,128)(2,1)S(1)} %broadcast_select_fusion.1), channel_id=1, source_target_pairs={{16,0},{20,4},{24,8},{28,12},{0,16},{4,20},{8,24},{12,28},{17,1},{... | collective-permute-start | bytes 884744 | tf_op jit(solution)/shard_map/while/body/eval_jaxpr/ppermute | solution.py:11
  49.1 164.8 %all-reduce.3.cloned.1.call-start = ((), (), s32[]{:S(2)}) async-start(), calls=%async_computation.2 | async-start | bytes 4456448 | tf_op jit(solution)/shard_map/psum | solution.py:101
  73.0 2.9 %copy-start.3 = (f32[64,192]{1,0:T(8,128)}, f32[64,192]{1,0:T(8,128)S(1)}, u32[]{:S(2)}) copy-start(f32[64,192]{1,0:T(8,128)S(1)} %broadcast_multiply_fusion) | copy-start | bytes 147460
  213.9 3.1 %copy-start.4 = (f32[512,64]{0,1:T(8,128)S(1)}, f32[512,64]{0,1:T(8,128)}, u32[]{:S(2)}) copy-start(f32[512,64]{0,1:T(8,128)} %get-tuple-element.40) | copy-start | bytes 393220
Sparse Core Ops, SparseCore 0:
  49.2 22.7 reduce-scatter.3
  78.1 135.7 all-reduce.2
where the time goes:
time: 225 us; the launch traced here: 224 us
  waiting for transfers between devices  146 us (65%)
  blocking collectives  39.6 us (18%)
  between operations  14.2 us (6%)
  matrix products  8.95 us (4%)
  starting transfers between devices  8.36 us (4%)
  local copies, waits for them, and re-layouts  7.02 us (3%)
    psum x1, waiting for transfers between devices, on_device(): lax.psum((term_w_in, term_b_in, term_w_out), ('blk', 'rep'))  98.3 us
    psum x1, blocking collectives, on_device(): lax.psum((term_w_in, term_b_in, term_w_out), ('blk', 'rep'))  39.6 us
    ppermute x3, waiting for transfers between devices, shifted(): return lax.ppermute(block, axis, route)  24.8 us
    unnamed x3, waiting for transfers between devices  22.9 us
    ppermute x3, starting transfers between devices, shifted(): return lax.ppermute(block, axis, route)  8.29 us
    unnamed x19, local copies, waits for them, and re-layouts  7.01 us
  transfers between devices with their start and end apart: 5, of which 5 were waited for; matrix products, arithmetic and copies ran while one was open for 1% of the time, Pallas kernels for 0%

commit v1 on v0

--- a/solution.py
+++ b/solution.py
@@ -1,8 +1,18 @@
+import functools
 import math
 import jax
 import jax.numpy as jnp
 from jax import lax
 from jax.sharding import PartitionSpec as P
+
+
+def resolve_zones(local_values, net_axis, axis_tag):
+    for d in (net_axis, axis_tag):
+        local_values = lax.psum(local_values, d)
+    return local_values
+
+
+end_the_rates = functools.partial(resolve_zones, net_axis="rep", axis_tag="blk")
 
 
 def shifted(block, axis, distance):
@@ -98,7 +108,7 @@
         )
         * norm
     )
-    grad_w_in, grad_b_in, grad_w_out = lax.psum((term_w_in, term_b_in, term_w_out), ("blk", "rep"))
+    grad_w_in, grad_b_in, grad_w_out = end_the_rates((term_w_in, term_b_in, term_w_out))
     return (feat_grad, grad_w_in, grad_b_in, grad_w_out)
 
 

time: 225 us -> 250 us (1.11)
  waiting for transfers between devices: 146 us -> 183 us
  blocking collectives: 39.6 us -> 28.6 us
    psum x1 -> x2, waiting for transfers between devices: 98.3 us -> 135 us  [resolve_zones(): local_values = lax.psum(local_values, d)]
    psum x1 -> x2, blocking collectives: 39.6 us -> 28.6 us  [resolve_zones(): local_values = lax.psum(local_values, d)]
    unnamed x3 -> x4, waiting for transfers between devices: 22.9 us -> 22.9 us
  transfers between devices with their start and end apart: 5 -> 6, of which waited for: 5 -> 6; matrix products, arithmetic and copies ran while one was open for 1% -> 1% of each run, Pallas kernels for 0% -> 0%
where the time goes in v1:
time: 250 us
  waiting for transfers between devices  183 us (73%)
  blocking collectives  28.6 us (11%)
  between operations  13.9 us (6%)
  matrix products  8.95 us (4%)
  starting transfers between devices  8.41 us (3%)
  local copies, waits for them, and re-layouts  7.02 us (3%)
    psum x2, waiting for transfers between devices, resolve_zones(): local_values = lax.psum(local_values, d)  135 us
    psum x2, blocking collectives, resolve_zones(): local_values = lax.psum(local_values, d)  28.6 us
    ppermute x3, waiting for transfers between devices, shifted(): return lax.ppermute(block, axis, route)  24.8 us
    unnamed x4, waiting for transfers between devices  22.9 us
    ppermute x3, starting transfers between devices, shifted(): return lax.ppermute(block, axis, route)  8.29 us
    unnamed x19, local copies, waits for them, and re-layouts  7.01 us
  transfers between devices with their start and end apart: 6, of which 6 were waited for; matrix products, arithmetic and copies ran while one was open for 1% of the time, Pallas kernels for 0%

profile of v1, /device:TPU:0, one launch (start us, length us, event | category | flops | bytes accessed | tf_op | source)
XLA Modules:
  0.0 249.8 jit_solution(6843363047166773124)
XLA Ops:
  7.2 0.0 reduce-scatter.4.cloned.1.call-start
  7.3 1.3 copy-done
  8.6 2.2 tanh_convert_fusion
  10.8 0.4 fusion.3
  11.2 6.1 %collective-permute-start = (bf16[192,768]{1,0:T(8,128)(2,1)S(1)}, bf16[192,768]{1,0:T(8,128)(2,1)S(1)}, u32[]{:S(2)}, u32[]{:S(2)}) collective-permute-start(bf16[192,768]{1,0:T(8,128)(2,1)S(1)} %pad_maximum_fusion), channel_id=1, source_target_pairs={{4,0},{8,4},{12,8},{16,12},{20,16},{24,20},{28,24},{0,28},{5,1},{9... | collective-permute-start | bytes 884744 | tf_op jit(solution)/shard_map/ppermute | solution.py:21
  17.3 6.3 %collective-permute-done = bf16[192,768]{1,0:T(8,128)(2,1)S(1)} collective-permute-done((bf16[192,768]{1,0:T(8,128)(2,1)S(1)}, bf16[192,768]{1,0:T(8,128)(2,1)S(1)}, u32[]{:S(2)}, u32[]{:S(2)}) %collective-permute-start) | collective-permute-done | bytes 294944 | tf_op jit(solution)/shard_map/ppermute | solution.py:21
  23.6 0.1 broadcast_select_fusion
  23.6 1.6 collective-permute-start.1
  25.3 6.3 %collective-permute-done.1 = bf16[192,768]{1,0:T(8,128)(2,1)S(1)} collective-permute-done((bf16[192,768]{1,0:T(8,128)(2,1)S(1)}, bf16[192,768]{1,0:T(8,128)(2,1)S(1)}, u32[]{:S(2)}, u32[]{:S(2)}) %collective-permute-start.1) | collective-permute-done | bytes 294944 | tf_op jit(solution)/shard_map/ppermute | solution.py:21
  31.6 0.6 collective-permute-start.2
  32.3 0.5 fusion.13
  32.8 0.9 convert_reduce_fusion.1
  33.7 12.2 %collective-permute-done.2 = bf16[192,768]{1,0:T(8,128)(2,1)S(1)} collective-permute-done((bf16[192,768]{1,0:T(8,128)(2,1)S(1)}, bf16[192,768]{1,0:T(8,128)(2,1)S(1)}, u32[]{:S(2)}, u32[]{:S(2)}) %collective-permute-start.2) | collective-permute-done | bytes 294944 | tf_op jit(solution)/shard_map/while/body/eval_jaxpr/ppermute | solution.py:21
  46.0 0.5 fusion.10
  46.5 0.9 convert_reduce_fusion
  47.4 0.3 fusion.8
  47.8 0.3 fusion
  48.1 0.9 copy.11
  49.1 0.0 all-reduce.7.cloned.1.call-start
  49.1 22.9 %reduce-scatter.4.cloned.1.call-done = f32[192,64]{1,0:T(8,128)} async-done(((f32[768,64]{1,0:T(8,128)}), f32[192,64]{1,0:T(8,128)}) %reduce-scatter.4.cloned.1.call-update) | async-done | bytes 49168
  72.0 1.0 copy.12
  73.0 0.1 broadcast_multiply_fusion
  73.0 0.3 fusion.19
  73.3 0.8 convolution_multiply_fusion.3
  74.1 1.8 convolution_multiply_fusion
  75.9 0.0 all-reduce.5.cloned.1.call-start
  76.0 53.6 %all-reduce.7.cloned.1.call-done = (f32[1024,512]{1,0:T(8,128)}, f32[512,64]{0,1:T(8,128)}) async-done(((f32[1024,512]{1,0:T(8,128)}, f32[512,64]{0,1:T(8,128)}), (f32[1024,512]{1,0:T(8,128)}, f32[512,64]{0,1:T(8,128)})) %all-reduce.7.cloned.1.call-update) | async-done | bytes 2228240 | tf_op jit(solution)/shard_map/psum | solution.py:11
  129.7 5.8 %psum.44 = f32[512]{0:T(512)S(1)} all-reduce(f32[512]{0:T(512)S(1)} %broadcast_multiply_fusion.1), channel_id=1, replica_groups=mesh['blk'=8,'rep'=4] {'rep'}, use_global_device_ids=true, to_apply=%region_9.10 | all-reduce | flops 512 | bytes 4096 | tf_op jit(solution)/shard_map/psum | solution.py:11
  135.5 22.8 %psum.45 = f32[512]{0:T(512)} all-reduce(f32[512]{0:T(512)S(1)} %psum.44), channel_id=1, replica_groups=mesh['blk'=8,'rep'=4] {'blk'}, use_global_device_ids=true, to_apply=%region_10.11 | all-reduce | flops 512 | bytes 4096 | tf_op jit(solution)/shard_map/psum | solution.py:11
  158.3 81.2 %all-reduce.5.cloned.1.call-done = (f32[1024,512]{1,0:T(8,128)}, f32[512,64]{0,1:T(8,128)}) async-done(((f32[1024,512]{1,0:T(8,128)}, f32[512,64]{0,1:T(8,128)}), (f32[1024,512]{1,0:T(8,128)}, f32[512,64]{0,1:T(8,128)})) %all-reduce.5.cloned.1.call-update) | async-done | bytes 2228240 | tf_op jit(solution)/shard_map/psum | solution.py:11
  239.5 3.1 %copy.18 = f32[1024,512]{1,0:T(8,128)} copy(f32[1024,512]{1,0:T(8,128)} %get-tuple-element.40) | data formatting | bytes 4194304
  242.6 0.7 copy.19
  (24 shorter events, 0.2 us)
Async XLA Ops:
  7.2 1.4 copy-start
  7.2 3.6 %copy-start.6 = (f32[64]{0:T(128)S(1)}, f32[64]{0:T(128)}, u32[]{:S(2)}) copy-start(f32[64]{0:T(128)} %param.11) | copy-start | bytes 772
  7.2 3.6 %copy-start.5 = (bf16[512,64]{0,1:T(8,128)(2,1)S(1)}, bf16[512,64]{0,1:T(8,128)(2,1)}, u32[]{:S(2)}) copy-start(bf16[512,64]{0,1:T(8,128)(2,1)} %param.10) | copy-start | bytes 196612
  7.2 4.0 %copy-start.1 = (bf16[64,768]{1,0:T(8,128)(2,1)S(1)}, bf16[64,768]{1,0:T(8,128)(2,1)}, u32[]{:S(2)}) copy-start(bf16[64,768]{1,0:T(8,128)(2,1)} %param.12) | copy-start | bytes 294916
  7.2 4.0 %copy-start.2 = (bf16[64,768]{1,0:T(8,128)(2,1)S(1)}, bf16[64,768]{1,0:T(8,128)(2,1)}, u32[]{:S(2)}) copy-start(bf16[64,768]{1,0:T(8,128)(2,1)} %param.13) | copy-start | bytes 294916
  7.2 64.8 %reduce-scatter.4.cloned.1.call-start = ((), (), s32[]{:S(2)}) async-start(), calls=%async_computation.1 | async-start | bytes 491520
  11.2 12.3 %collective-permute-start = (bf16[192,768]{1,0:T(8,128)(2,1)S(1)}, bf16[192,768]{1,0:T(8,128)(2,1)S(1)}, u32[]{:S(2)}, u32[]{:S(2)}) collective-permute-start(bf16[192,768]{1,0:T(8,128)(2,1)S(1)} %pad_maximum_fusion), channel_id=1, source_target_pairs={{4,0},{8,4},{12,8},{16,12},{20,16},{24,20},{28,24},{0,28},{5,1},{9... | collective-permute-start | bytes 884744 | tf_op jit(solution)/shard_map/ppermute | solution.py:21
  23.6 7.9 %collective-permute-start.1 = (bf16[192,768]{1,0:T(8,128)(2,1)S(1)}, bf16[192,768]{1,0:T(8,128)(2,1)S(1)}, u32[]{:S(2)}, u32[]{:S(2)}) collective-permute-start(bf16[192,768]{1,0:T(8,128)(2,1)S(1)} %broadcast_select_fusion), channel_id=1, source_target_pairs={{8,0},{12,4},{16,8},{20,12},{24,16},{28,20},{0,24},{4,28},{9,1},{1... | collective-permute-start | bytes 884744 | tf_op jit(solution)/shard_map/ppermute | solution.py:21
  31.6 14.3 %collective-permute-start.2 = (bf16[192,768]{1,0:T(8,128)(2,1)S(1)}, bf16[192,768]{1,0:T(8,128)(2,1)S(1)}, u32[]{:S(2)}, u32[]{:S(2)}) collective-permute-start(bf16[192,768]{1,0:T(8,128)(2,1)S(1)} %broadcast_select_fusion.1), channel_id=1, source_target_pairs={{16,0},{20,4},{24,8},{28,12},{0,16},{4,20},{8,24},{12,28},{17,1},{... | collective-permute-start | bytes 884744 | tf_op jit(solution)/shard_map/while/body/eval_jaxpr/ppermute | solution.py:21
  49.1 80.6 %all-reduce.7.cloned.1.call-start = ((), (), s32[]{:S(2)}) async-start(), calls=%async_computation.3 | async-start | bytes 4456448 | tf_op jit(solution)/shard_map/psum | solution.py:11
  73.0 2.9 %copy-start.3 = (f32[64,192]{1,0:T(8,128)}, f32[64,192]{1,0:T(8,128)S(1)}, u32[]{:S(2)}) copy-start(f32[64,192]{1,0:T(8,128)S(1)} %broadcast_multiply_fusion) | copy-start | bytes 147460
  75.9 163.6 %all-reduce.5.cloned.1.call-start = ((), (), s32[]{:S(2)}) async-start(), calls=%async_computation.2 | async-start | bytes 4456448 | tf_op jit(solution)/shard_map/psum | solution.py:11
  239.5 3.1 %copy-start.4 = (f32[512,64]{0,1:T(8,128)S(1)}, f32[512,64]{0,1:T(8,128)}, u32[]{:S(2)}) copy-start(f32[512,64]{0,1:T(8,128)} %get-tuple-element.42) | copy-start | bytes 393220
Sparse Core Ops, SparseCore 0:
  49.2 22.7 reduce-scatter.3
  76.1 53.5 all-reduce.6
  133.3 106.1 all-reduce.4
